TPU v7x, 32 devices: a whole 2x2x4 slice. The times are simulated.
32 devices in a mesh: scene: 4 (over x, core), view: 4 (over z), half: 2 (over y).
Axes of the slice: x: 2, y: 2, z: 4, core: 2. Of those that a mesh axis runs over, the one named last changes fastest.
Arguments:
- tokens: bfloat16 [16, 512, 2048], P(('scene', 'view'), 'half'), parts along dimension 0, may hold values from -9 to 12
- w_qkv: bfloat16 [2048, 768], replicated, may hold values from -0.125 to 0.125
- w_out: bfloat16 [256, 2048], replicated, may hold values from -5 to 5
- key_lists: int32 [16, 4, 2], P(('scene', 'view'), 'half'), parts along dimension 0, may hold values from 0 to 15, as said below
- list_len: int32 [16, 4], P(('scene', 'view'), 'half'), parts along dimension 0, may hold values from 1 to 2, as said below
Outputs:
- mixed: bfloat16 [16, 512, 2048], P(('scene', 'view'), 'half'), parts along dimension 0
There are 4 independent parts, one for each index of `scene`. A program takes and returns all parts, laid end to end along the dimension named above; an argument that names none is the same for every part. Nothing has to cross between parts.
Inputs may be any that keep to these rules, and one draw needn't show every extreme that they name: `key_lists`: entries of one list are distinct block ids of the scene. `list_len`: some query block lists 2 blocks in every scene.
All inputs are finite; a program needn't handle non-finite values.
Results may differ from a plain program's by a relative error of at most 0.014.
The roundings to bfloat16 on the way count: a program that leaves them out, or rounds other values in their place, can miss the bound.
Values may be sent and summed in bfloat16 or wider, within the bound.
A program may use at most 64 MiB of HBM per device.

v0:
```python
import jax
import jax.numpy as jnp
from jax import lax
from jax.sharding import PartitionSpec as P

HEADS = 4
NEG = -1e30


def block_mask(lists, lengths, count, block):
    key_rows = jnp.arange(count, dtype=jnp.int32)
    key_block = key_rows // block
    slots = jnp.arange(lists.shape[1], dtype=jnp.int32)
    live = slots[None, :] < lengths[:, None]
    hits = (lists[:, :, None] == key_block[None, None, :]) & live[:, :, None]
    return jnp.any(hits, axis=1)


def attend(state, queries, keys, values, allowed):
    peak, total, accum = state
    heads = accum.shape[1]
    q3 = queries.reshape(queries.shape[0], heads, -1)
    k3 = keys.reshape(keys.shape[0], heads, -1)
    v3 = values.reshape(values.shape[0], heads, -1)
    scores = jnp.einsum("qhd,khd->hqk", q3, k3, preferred_element_type=jnp.float32) * q3.shape[
        2
    ] ** (-0.5)
    masked = jnp.where(allowed[None], scores, NEG)
    fresh = jnp.maximum(peak, jnp.max(masked, axis=2))
    weights = jnp.where(allowed[None], jnp.exp(scores - fresh[:, :, None]), 0.0)
    factor = jnp.exp(peak - fresh)
    total = jnp.sum(weights, axis=2)
    summed = jnp.einsum(
        "hqk,khd->qhd", weights.astype(jnp.bfloat16), v3, preferred_element_type=jnp.float32
    )
    accum = accum * factor.T[:, :, None] + summed
    return (fresh, total, accum)


def visit(state, queries, keys, values, allowed):
    return lax.cond(
        jnp.any(allowed),
        lambda held: attend(held, queries, keys, values, allowed),
        lambda held: held,
        state,
    )


def per_device(tokens, w_qkv, w_out, key_lists, list_len):
    rows = tokens.shape[1]
    width = tokens.shape[2]
    flat = tokens.reshape(rows, width)
    inner = w_out.shape[0]
    head_size = inner // HEADS
    proj = jnp.dot(flat, w_qkv, preferred_element_type=jnp.float32).astype(jnp.bfloat16)
    queries = proj[:, :inner]
    keys = proj[:, inner : 2 * inner]
    values = proj[:, 2 * inner :]
    lists = key_lists.reshape(-1, key_lists.shape[2])
    lengths = list_len.reshape(-1)
    local_blocks = lists.shape[0]
    block = rows // local_blocks
    peak0 = jnp.full((HEADS, rows), NEG, jnp.float32)
    total0 = jnp.zeros((HEADS, rows), jnp.float32)
    accum0 = jnp.zeros((rows, HEADS, head_size), jnp.float32)
    view_keys, view_values = (
        lax.all_gather(keys, "half", axis=0, tiled=True),
        lax.all_gather(values, "half", axis=0, tiled=True),
    )
    piece = (
        lax.all_gather(view_keys, "view", axis=0, tiled=True),
        lax.all_gather(view_values, "view", axis=0, tiled=True),
    )
    count = piece[0].shape[0]
    allowed = jnp.repeat(block_mask(lists, lengths, count, block), block, axis=0)
    peak, total, accum = visit((peak0, total0, accum0), queries, piece[0], piece[1], allowed)
    attn = (accum / total.T[:, :, None]).reshape(rows, inner).astype(jnp.bfloat16)
    mixed = jnp.dot(attn, w_out, preferred_element_type=jnp.float32).astype(jnp.bfloat16)
    return mixed.reshape(1, rows, width)


def solution(mesh):
    placed = (
        P(("scene", "view"), "half", None),
        P(),
        P(),
        P(("scene", "view"), "half", None),
        P(("scene", "view"), "half"),
    )
    return jax.shard_map(
        per_device,
        mesh=mesh,
        in_specs=placed,
        out_specs=P(("scene", "view"), "half", None),
        check_vma=False,
    )
```

profile of v0, /device:TPU:0, one launch (start us, length us, event | category | flops | bytes accessed | tf_op | source)
XLA Modules:
  0.0 109.8 jit_solution(13672634810469193445)
XLA Ops:
  6.5 0.0 copy-start
  6.5 0.0 all-gather.3.cloned.1.call-start
  6.5 1.9 %copy-done = bf16[2048,768]{1,0:T(8,128)(2,1)S(1)} copy-done((bf16[2048,768]{1,0:T(8,128)(2,1)S(1)}, bf16[2048,768]{1,0:T(8,128)(2,1)}, u32[]{:S(2)}) %copy-start) | copy-done | bytes 3145752
  8.4 2.2 %convolution_convert_fusion.1 = bf16[256,768]{1,0:T(8,128)(2,1)S(1)} fusion(bf16[2048,768]{1,0:T(8,128)(2,1)S(1)} %copy-done, bf16[1,256,2048]{2,1,0:T(8,128)(2,1)} %param.7), kind=kOutput, calls=%fused_computation.14 | convolution fusion | flops 805502976 | bytes 4587520 | tf_op jit(solution)/shard_map/dot_general | solution.py:55
  10.6 0.7 fusion.18
  11.3 7.2 %all_gather.12 = bf16[512,256]{1,0:T(8,128)(2,1)} all-gather(bf16[256,256]{1,0:T(8,128)(2,1)S(1)} %get-tuple-element.35), channel_id=1, replica_groups=mesh['scene'=4,'view'=4,'half'=2] {'half'}, dimensions={0}, use_global_device_ids=true | all-gather | bytes 393216 | tf_op jit(solution)/shard_map/all_gather | solution.py:67
  18.5 0.0 all-gather.3.cloned.1.call-update
  18.6 0.0 all-gather.5.cloned.1.call-start
  18.6 7.2 %all_gather.14 = bf16[512,256]{1,0:T(8,128)(2,1)} all-gather(bf16[256,256]{1,0:T(8,128)(2,1)} %get-tuple-element.34), channel_id=1, replica_groups=mesh['scene'=4,'view'=4,'half'=2] {'half'}, dimensions={0}, use_global_device_ids=true | all-gather | bytes 393216 | tf_op jit(solution)/shard_map/all_gather | solution.py:68
  25.8 0.0 all-gather.5.cloned.1.call-update
  25.9 0.7 iota_compare_fusion
  26.6 0.8 and_reduce_fusion
  27.4 1.2 %broadcast_reduce_fusion = pred[]{:T(512)} fusion(pred[2,2048]{1,0:T(4,128)(4,1)S(1)} %and_reduce_fusion), kind=kLoop, calls=%fused_computation.16 | loop fusion | flops 524287 | bytes 4097 | tf_op jit(solution)/shard_map/reduce_or | solution.py:42
  29.2 19.0 %all-gather.3.cloned.1.call-done = bf16[2048,256]{1,0:T(8,128)(2,1)} async-done(((bf16[512,256]{1,0:T(8,128)(2,1)}), bf16[2048,256]{1,0:T(8,128)(2,1)}) %all-gather.3.cloned.1.call-update) | async-done | bytes 1048592 | tf_op jit(solution)/shard_map/all_gather | solution.py:71
  48.2 28.9 %all-gather.5.cloned.1.call-done = bf16[2048,256]{1,0:T(8,128)(2,1)} async-done(((bf16[512,256]{1,0:T(8,128)(2,1)}), bf16[2048,256]{1,0:T(8,128)(2,1)}) %all-gather.5.cloned.1.call-update) | async-done | bytes 1048592 | tf_op jit(solution)/shard_map/all_gather | solution.py:72
  77.1 1.0 broadcast_in_dim.41
  78.2 22.1 %conditional.1 = (f32[4,256]{1,0:T(4,128)S(1)}, f32[256,4,64]{0,2,1:T(8,128)S(1)}) conditional(s32[]{:T(128)} %convert_element_type.18, () %tuple.13, (pred[2,128,2048]{2,1,0:T(8,128)(4,1)}, bf16[256,768]{1,0:T(8,128)(2,1)S(1)}, bf16[2048,256]{1,0:T(8,128)(2,1)}, bf16[2048,256]{1,0:T(8,128)(2,1)}) %tuple.14), branch_computations={%region_2.3_spmd, %region_3.6_spmd} | conditional | flops 560006144 | bytes 68059184 | solution.py:41
  78.2 2.3 %copy.10 = bf16[2048,256]{0,1:T(8,128)(2,1)} copy(bf16[2048,256]{1,0:T(8,128)(2,1)} %get-tuple-element.28) | data formatting | bytes 2097152 | tf_op jit(solution)/shard_map
  80.4 0.9 copy.9
  81.3 0.9 slice.12
  82.3 6.2 %select_reduce_fusion = (f32[4,256]{1,0:T(4,128)S(1)}, f32[4,256,2048]{2,1,0:T(8,128)}) fusion(pred[256,2048]{1,0:T(8,128)(4,1)} %bitcast, bf16[256,4,64]{0,2,1:T(8,128)(2,1)S(1)} %bitcast.27, bf16[2048,4,64]{0,2,1:T(8,128)(2,1)} %bitcast.25), kind=kOutput, calls=%fused_computation.1 | convolution fusion | flops 274725888 | bytes 10096640 | tf_op jit(solution)/shard_map/cond/branch_1_fun/qhd,khd->hqk/dot_general | solution.py:25
  88.5 2.3 %copy.11 = bf16[2048,256]{0,1:T(8,128)(2,1)} copy(bf16[2048,256]{1,0:T(8,128)(2,1)} %get-tuple-element.29) | data formatting | bytes 2097152 | tf_op jit(solution)/shard_map
  90.8 0.0 copy-start.1
  90.8 5.2 %fusion.8 = f32[256,4,64]{0,2,1:T(8,128)S(1)} fusion(bf16[2048,4,64]{0,2,1:T(8,128)(2,1)} %bitcast.26, f32[4,256,2048]{2,1,0:T(8,128)} %get-tuple-element.33, f32[4,256]{1,0:T(4,128)S(1)} %get-tuple-element.31, pred[256,2048]{1,0:T(8,128)(4,1)} %bitcast, f32[256,4]{0,1:T(4,128)S(1)} %get-tuple-element.30), kind=kOutput, calls=%fused_computation.7 | convolution fusion | flops 276889600 | bytes 10231808 | tf_op jit(solution)/shard_map/cond/branch_1_fun/hqk,khd->qhd/dot_general | solution.py:33
  96.0 1.1 %copy-done.1 = f32[4,256,2048]{2,1,0:T(8,128)S(1)} copy-done((f32[4,256,2048]{2,1,0:T(8,128)S(1)}, f32[4,256,2048]{2,1,0:T(8,128)}, u32[]{:S(2)}) %copy-start.1) | copy-done | bytes 8388632 | tf_op jit(solution)/shard_map/cond
  97.1 3.2 %fusion.1 = f32[4,256]{1,0:T(4,128)S(1)} fusion(f32[4,256,2048]{2,1,0:T(8,128)S(1)} %copy-done.1, f32[4,256]{1,0:T(4,128)S(1)} %get-tuple-element.31, pred[256,2048]{1,0:T(8,128)(4,1)} %bitcast), kind=kLoop, calls=%fused_computation.3 | loop fusion | flops 8387584 | bytes 8921088 | tf_op jit(solution)/shard_map/cond/branch_1_fun/reduce_sum | solution.py:32
  100.3 2.7 %fusion.13 = bf16[1,256,2048]{2,1,0:T(8,128)(2,1)} fusion(bf16[256,256]{0,1:T(8,128)(2,1)S(1)} %bitcast.28, bf16[256,2048]{1,0:T(8,128)(2,1)} %param.9), kind=kOutput, calls=%fused_computation.13 | convolution fusion | flops 268959744 | bytes 2228224 | tf_op jit(solution)/shard_map/dot_general | solution.py:78
  (3 shorter events, 0.0 us)
Async XLA Ops:
  6.5 1.9 %copy-start = (bf16[2048,768]{1,0:T(8,128)(2,1)S(1)}, bf16[2048,768]{1,0:T(8,128)(2,1)}, u32[]{:S(2)}) copy-start(bf16[2048,768]{1,0:T(8,128)(2,1)} %param.8) | copy-start | bytes 9437188
  6.5 41.7 %all-gather.3.cloned.1.call-start = ((), (), s32[]{:S(2)}) async-start(), calls=%async_computation | async-start | bytes 1310720 | tf_op jit(solution)/shard_map/all_gather | solution.py:71
  18.6 58.6 %all-gather.5.cloned.1.call-start = ((), (), s32[]{:S(2)}) async-start(), calls=%async_computation.1 | async-start | bytes 1310720 | tf_op jit(solution)/shard_map/all_gather | solution.py:72
  90.8 6.3 %copy-start.1 = (f32[4,256,2048]{2,1,0:T(8,128)S(1)}, f32[4,256,2048]{2,1,0:T(8,128)}, u32[]{:S(2)}) copy-start(f32[4,256,2048]{2,1,0:T(8,128)} %get-tuple-element.33) | copy-start | bytes 25165828 | tf_op jit(solution)/shard_map/cond
Sparse Core Ops, SparseCore 0:
  18.7 29.4 all-gather.2
  49.8 27.3 all-gather.4
where the time goes:
time: 110 us
  waiting for transfers between devices  47.9 us (44%)
  matrix products  16.3 us (15%)
  blocking collectives  14.4 us (13%)
  between operations  14.1 us (13%)
  local copies, waits for them, and re-layouts  11.1 us (10%)
  other arithmetic  5.97 us (5%)
    all_gather x1, waiting for transfers between devices, per_device(): lax.all_gather(view_values, 'view', axis=0, tiled=True)  28.9 us
    all_gather x1, waiting for transfers between devices, per_device(): lax.all_gather(view_keys, 'view', axis=0, tiled=True)  19 us
    all_gather x1, blocking collectives, per_device(): lax.all_gather(keys, 'half', axis=0, tiled=True)  7.24 us
    all_gather x1, blocking collectives, per_device(): lax.all_gather(values, 'half', axis=0, tiled=True)  7.21 us
    dot_general x1, matrix products, attend(): jnp.einsum('qhd,khd->hqk', q3, k3, preferred_element_type=jnp.float32)  6.24 us
    another operation x3, local copies, waits for them, and re-layouts  5.44 us
    dot_general x1, matrix products, attend(): jnp.einsum('hqk,khd->qhd', weights.astype(jnp.bfloat16), v3, preferred_el...  5.18 us
    reduce_sum x1, other arithmetic, attend(): total = jnp.sum(weights, axis=2)  3.21 us
  transfers between devices with their start and end apart: 2, of which 2 were waited for; matrix products, arithmetic and copies ran while one was open for 2% of the time, Pallas kernels for 0%

commit v1 on v0

--- a/solution.py
+++ b/solution.py
@@ -5,6 +5,29 @@
 
 HEADS = 4
 NEG = -1e30
+
+
+def arrange_stocks(local_array, dimension_no):
+    prior = list(local_array.shape[1:])
+    prior[dimension_no] *= local_array.shape[0]
+    return jnp.moveaxis(local_array, 0, dimension_no).reshape(prior)
+
+
+def _turn_tiles(page, group_axis):
+    u_next = lax.axis_size(group_axis)
+    all_values = lax.axis_index(group_axis)
+    arr_now, current_block = (u_next, all_values)
+    b_next, arr_next = (page[None], 1)
+    while arr_next < arr_now:
+        views = []
+        for at in tuple(range(arr_now)):
+            views.append((at, at ^ arr_next))
+        v_next = lax.ppermute(b_next, group_axis, perm=views)
+        v_now = current_block & arr_next == 0
+        big = jnp.where(v_now, b_next, v_next)
+        b_next = jnp.concatenate([big, jnp.where(v_now, v_next, b_next)])
+        arr_next *= 2
+    return b_next
 
 
 def block_mask(lists, lengths, count, block):
@@ -63,8 +86,13 @@
     peak0 = jnp.full((HEADS, rows), NEG, jnp.float32)
     total0 = jnp.zeros((HEADS, rows), jnp.float32)
     accum0 = jnp.zeros((rows, HEADS, head_size), jnp.float32)
+
+    def watch_the_kinds(xx, tile_in, array_axis=0):
+        state_now = _turn_tiles(xx, tile_in)
+        return arrange_stocks(state_now, array_axis)
+
     view_keys, view_values = (
-        lax.all_gather(keys, "half", axis=0, tiled=True),
+        watch_the_kinds(keys, "half"),
         lax.all_gather(values, "half", axis=0, tiled=True),
     )
     piece = (

time: 110 us -> 102 us (0.927)
  blocking collectives: 14.4 us -> 7.24 us
  matrix products: 16.3 us -> 10.9 us
  waiting for transfers between devices: 47.9 us -> 51.2 us
  starting transfers between devices: 0.04 us -> 1.86 us
  local copies, waits for them, and re-layouts: 11.1 us -> 9.55 us
    all_gather x1, waiting for transfers between devices: 28.9 us -> 18.7 us  [per_device(): lax.all_gather(view_values, 'view', axis=0, tiled=True)]
    all_gather x1, waiting for transfers between devices: 19 us -> 29 us  [per_device(): lax.all_gather(view_keys, 'view', axis=0, tiled=True)]
    all_gather x1 -> x0, blocking collectives: 7.24 us -> none  [per_device(): lax.all_gather(keys, 'half', axis=0, tiled=True)]
    ppermute x0 -> x1, waiting for transfers between devices: none -> 3.53 us  [_turn_tiles(): v_next = lax.ppermute(b_next, group_axis, perm=views)]
    dot_general x1, matrix products: 6.24 us -> 3.14 us  [attend(): jnp.einsum('qhd,khd->hqk', q3, k3, preferred_element_type=jnp.float32)]
    dot_general x1, matrix products: 5.18 us -> 2.87 us  [attend(): jnp.einsum('hqk,khd->qhd', weights.astype(jnp.bfloat16), v3, preferred_el...]
    another operation x3 -> x2, local copies, waits for them, and re-layouts: 5.44 us -> 3.19 us
    ppermute x0 -> x1, starting transfers between devices: none -> 1.82 us  [_turn_tiles(): v_next = lax.ppermute(b_next, group_axis, perm=views)]
  transfers between devices with their start and end apart: 2 -> 3, of which waited for: 2 -> 3; matrix products, arithmetic and copies ran while one was open for 2% -> 5% of each run, Pallas kernels for 0% -> 0%
where the time goes in v1:
time: 102 us; the launch traced here: 101 us
  waiting for transfers between devices  51.2 us (50%)
  between operations  14.1 us (14%)
  matrix products  10.9 us (11%)
  local copies, waits for them, and re-layouts  9.55 us (9%)
  blocking collectives  7.24 us (7%)
  other arithmetic  6.29 us (6%)
  starting transfers between devices  1.86 us (2%)
    all_gather x1, waiting for transfers between devices, per_device(): lax.all_gather(view_keys, 'view', axis=0, tiled=True)  29 us
    all_gather x1, waiting for transfers between devices, per_device(): lax.all_gather(view_values, 'view', axis=0, tiled=True)  18.7 us
    all_gather x1, blocking collectives, per_device(): lax.all_gather(values, 'half', axis=0, tiled=True)  7.24 us
    ppermute x1, waiting for transfers between devices, _turn_tiles(): v_next = lax.ppermute(b_next, group_axis, perm=views)  3.53 us
    reduce_sum x1, other arithmetic, attend(): total = jnp.sum(weights, axis=2)  3.22 us
    another operation x2, local copies, waits for them, and re-layouts  3.19 us
    dot_general x1, matrix products, attend(): jnp.einsum('qhd,khd->hqk', q3, k3, preferred_element_type=jnp.float32)  3.14 us
    dot_general x1, matrix products, attend(): jnp.einsum('hqk,khd->qhd', weights.astype(jnp.bfloat16), v3, preferred_el...  2.87 us
  transfers between devices with their start and end apart: 3, of which 3 were waited for; matrix products, arithmetic and copies ran while one was open for 5% of the time, Pallas kernels for 0%

profile of v1, /device:TPU:0, one launch (start us, length us, event | category | flops | bytes accessed | tf_op | source)
XLA Modules:
  0.0 101.2 jit_solution(2738784510463417492)
XLA Ops:
  6.5 0.0 copy-start
  6.5 0.0 copy-start.3
  6.5 0.0 all-gather.5.cloned.1.call-start
  6.5 1.9 %copy-done = bf16[2048,768]{1,0:T(8,128)(2,1)S(1)} copy-done((bf16[2048,768]{1,0:T(8,128)(2,1)S(1)}, bf16[2048,768]{1,0:T(8,128)(2,1)}, u32[]{:S(2)}) %copy-start) | copy-done | bytes 3145752
  8.4 2.2 %convolution_convert_fusion.1 = bf16[256,768]{1,0:T(8,128)(2,1)S(1)} fusion(bf16[2048,768]{1,0:T(8,128)(2,1)S(1)} %copy-done, bf16[1,256,2048]{2,1,0:T(8,128)(2,1)} %param.7), kind=kOutput, calls=%fused_computation.14 | convolution fusion | flops 805502976 | bytes 4587520 | tf_op jit(solution)/shard_map/dot_general | solution.py:78
  10.6 0.7 fusion.18
  11.3 7.2 %all_gather.10 = bf16[512,256]{1,0:T(8,128)(2,1)} all-gather(bf16[256,256]{1,0:T(8,128)(2,1)S(1)} %get-tuple-element.36), channel_id=1, replica_groups=mesh['scene'=4,'view'=4,'half'=2] {'half'}, dimensions={0}, use_global_device_ids=true | all-gather | bytes 393216 | tf_op jit(solution)/shard_map/all_gather | solution.py:96
  18.5 0.0 all-gather.5.cloned.1.call-update
  18.6 0.0 all-gather.3.cloned.1.call-start
  18.6 1.8 %collective-permute-start = (bf16[1,256,256]{2,1,0:T(8,128)(2,1)}, bf16[1,256,256]{2,1,0:T(8,128)(2,1)}, u32[]{:S(2)}, u32[]{:S(2)}) collective-permute-start(bf16[1,256,256]{2,1,0:T(8,128)(2,1)} %get-tuple-element.37), channel_id=1, source_target_pairs={{0,1},{1,0},{2,3},{3,2},{4,5},{5,4},{6,7},{7,6},{8,9},{9,8},{10,11... | collective-permute-start | bytes 393224 | tf_op jit(solution)/shard_map/ppermute | solution.py:25
  20.4 3.5 %collective-permute-done = bf16[1,256,256]{2,1,0:T(8,128)(2,1)} collective-permute-done((bf16[1,256,256]{2,1,0:T(8,128)(2,1)}, bf16[1,256,256]{2,1,0:T(8,128)(2,1)}, u32[]{:S(2)}, u32[]{:S(2)}) %collective-permute-start) | collective-permute-done | bytes 131104 | tf_op jit(solution)/shard_map/ppermute | solution.py:25
  24.0 0.9 broadcast_select_fusion.1
  24.9 0.7 pad_maximum_fusion
  25.6 1.8 %copy.9 = bf16[512,256]{0,1:T(8,128)(2,1)} copy(bf16[512,256]{1,0:T(8,128)(2,1)} %bitcast.34) | data formatting | bytes 524288 | tf_op jit(solution)/shard_map/reshape | solution.py:13
  27.4 0.0 all-gather.3.cloned.1.call-update
  27.5 0.0 copy-done.3
  27.5 0.1 iota_compare_fusion
  27.5 0.0 copy-done.2
  27.5 0.1 and_reduce_fusion
  27.7 1.2 %broadcast_reduce_fusion = pred[]{:T(512)} fusion(pred[2,2048]{1,0:T(4,128)(4,1)S(1)} %and_reduce_fusion), kind=kLoop, calls=%fused_computation.16 | loop fusion | flops 524287 | bytes 4097 | tf_op jit(solution)/shard_map/reduce_or | solution.py:65
  29.5 18.7 %all-gather.5.cloned.1.call-done = bf16[2048,256]{1,0:T(8,128)(2,1)} async-done(((bf16[512,256]{1,0:T(8,128)(2,1)}), bf16[2048,256]{1,0:T(8,128)(2,1)}) %all-gather.5.cloned.1.call-update) | async-done | bytes 1048592 | tf_op jit(solution)/shard_map/all_gather | solution.py:100
  48.2 29.0 %all-gather.3.cloned.1.call-done = bf16[2048,256]{0,1:T(8,128)(2,1)} async-done(((bf16[512,256]{0,1:T(8,128)(2,1)}), bf16[2048,256]{0,1:T(8,128)(2,1)}) %all-gather.3.cloned.1.call-update) | async-done | bytes 1048592 | tf_op jit(solution)/shard_map/all_gather | solution.py:99
  77.2 1.0 broadcast_in_dim.44
  78.2 13.5 %conditional.1 = (f32[4,256]{1,0:T(4,128)S(1)}, f32[256,4,64]{0,2,1:T(8,128)S(1)}) conditional(s32[]{:T(128)} %convert_element_type.18, () %tuple.13, (pred[2,128,2048]{2,1,0:T(8,128)(4,1)}, bf16[256,768]{1,0:T(8,128)(2,1)S(1)}, bf16[2048,256]{0,1:T(8,128)(2,1)}, bf16[2048,256]{1,0:T(8,128)(2,1)}) %tuple.14), branch_computations={%region_2.3_spmd, %region_3.6_spmd} | conditional | flops 560006144 | bytes 36601900 | solution.py:64
  78.2 2.3 %copy.11 = bf16[2048,256]{0,1:T(8,128)(2,1)} copy(bf16[2048,256]{1,0:T(8,128)(2,1)} %get-tuple-element.29) | data formatting | bytes 2097152 | tf_op jit(solution)/shard_map
  80.4 0.9 copy.10
  81.4 1.0 slice.12
  82.4 3.1 %select_reduce_fusion = (f32[4,256]{1,0:T(4,128)S(1)}, f32[4,256,2048]{2,1,0:T(8,128)S(1)}) fusion(pred[256,2048]{1,0:T(8,128)(4,1)} %bitcast, bf16[256,4,64]{0,2,1:T(8,128)(2,1)S(1)} %bitcast.35, bf16[2048,4,64]{0,2,1:T(8,128)(2,1)} %bitcast.32), kind=kOutput, calls=%fused_computation.1 | convolution fusion | flops 274725888 | bytes 10096640 | tf_op jit(solution)/shard_map/cond/branch_1_fun/qhd,khd->hqk/dot_general | solution.py:48
  85.5 0.0 copy-done.1
  85.5 2.9 %fusion.8 = f32[256,4,64]{0,2,1:T(8,128)S(1)} fusion(bf16[2048,4,64]{0,2,1:T(8,128)(2,1)S(1)} %bitcast.33, f32[4,256,2048]{2,1,0:T(8,128)S(1)} %get-tuple-element.33, f32[4,256]{1,0:T(4,128)S(1)} %get-tuple-element.31, pred[256,2048]{1,0:T(8,128)(4,1)} %bitcast, f32[256,4]{0,1:T(4,128)S(1)} %get-tuple-element.30), kind=kOutput, calls=%fused_computation.7 | convolution fusion | flops 276889600 | bytes 10231808 | tf_op jit(solution)/shard_map/cond/branch_1_fun/hqk,khd->qhd/dot_general | solution.py:56
  88.4 3.2 %fusion.1 = f32[4,256]{1,0:T(4,128)S(1)} fusion(f32[4,256,2048]{2,1,0:T(8,128)S(1)} %get-tuple-element.33, f32[4,256]{1,0:T(4,128)S(1)} %get-tuple-element.31, pred[256,2048]{1,0:T(8,128)(4,1)} %bitcast), kind=kLoop, calls=%fused_computation.3 | loop fusion | flops 8387584 | bytes 8921088 | tf_op jit(solution)/shard_map/cond/branch_1_fun/reduce_sum | solution.py:55
  91.7 2.7 %fusion.13 = bf16[1,256,2048]{2,1,0:T(8,128)(2,1)} fusion(bf16[256,256]{0,1:T(8,128)(2,1)S(1)} %bitcast.36, bf16[256,2048]{1,0:T(8,128)(2,1)} %param.9), kind=kOutput, calls=%fused_computation.13 | convolution fusion | flops 268959744 | bytes 2228224 | tf_op jit(solution)/shard_map/dot_general | solution.py:106
  (5 shorter events, 0.0 us)
Async XLA Ops:
  6.5 1.9 %copy-start = (bf16[2048,768]{1,0:T(8,128)(2,1)S(1)}, bf16[2048,768]{1,0:T(8,128)(2,1)}, u32[]{:S(2)}) copy-start(bf16[2048,768]{1,0:T(8,128)(2,1)} %param.8) | copy-start | bytes 9437188
  6.5 20.9 %copy-start.3 = (s32[1,2]{1,0:T(1,128)S(1)}, s32[1,2]{1,0:T(1,128)}, u32[]{:S(2)}) copy-start(s32[1,2]{1,0:T(1,128)} %param.11) | copy-start | bytes 28
  6.5 21.0 %copy-start.2 = (s32[1,2,2]{2,1,0:T(2,128)S(1)}, s32[1,2,2]{2,1,0:T(2,128)}, u32[]{:S(2)}) copy-start(s32[1,2,2]{2,1,0:T(2,128)} %param.10) | copy-start | bytes 52
  6.5 41.6 %all-gather.5.cloned.1.call-start = ((), (), s32[]{:S(2)}) async-start(), calls=%async_computation.1 | async-start | bytes 1310720 | tf_op jit(solution)/shard_map/all_gather | solution.py:100
  18.6 58.6 %all-gather.3.cloned.1.call-start = ((), (), s32[]{:S(2)}) async-start(), calls=%async_computation | async-start | bytes 1310720 | tf_op jit(solution)/shard_map/all_gather | solution.py:99
  18.6 5.3 %collective-permute-start = (bf16[1,256,256]{2,1,0:T(8,128)(2,1)}, bf16[1,256,256]{2,1,0:T(8,128)(2,1)}, u32[]{:S(2)}, u32[]{:S(2)}) collective-permute-start(bf16[1,256,256]{2,1,0:T(8,128)(2,1)} %get-tuple-element.37), channel_id=1, source_target_pairs={{0,1},{1,0},{2,3},{3,2},{4,5},{5,4},{6,7},{7,6},{8,9},{9,8},{10,11... | collective-permute-start | bytes 393224 | tf_op jit(solution)/shard_map/ppermute | solution.py:25
  81.4 4.2 %copy-start.1 = (bf16[2048,256]{0,1:T(8,128)(2,1)S(1)}, bf16[2048,256]{0,1:T(8,128)(2,1)}, u32[]{:S(2)}) copy-start(bf16[2048,256]{0,1:T(8,128)(2,1)} %copy.11) | copy-start | bytes 3145732 | tf_op jit(solution)/shard_map/cond
Sparse Core Ops, SparseCore 0:
  18.7 29.4 all-gather.4
  49.7 27.3 all-gather.2
